TPU v7x, 256 devices: a whole 4x4x8 slice. The times are simulated.
256 devices in a mesh: seq: 8 (over y, z_lo), exp: 32 (over x, z_hi, core).
Axes of the slice: x: 4, y: 4, z: 8 (z_hi: 4, z_lo: 2; z = z_hi * 2 + z_lo), core: 2. Of those that a mesh axis runs over, the one named last changes fastest.
Arguments:
- tokens: bfloat16 [16384, 4096], P(('seq', 'exp')), may hold values from -6 to 6
- norm_gain: float32 [4096], replicated, may hold values from 0.1 to 1.9
- queries: bfloat16 [16384, 2048], P(('seq', 'exp')), may hold values from -24 to 24
- attn_keys: bfloat16 [16384, 2048], P(('seq', 'exp')), may hold values from -4.5 to 4.5
- attn_values: bfloat16 [16384, 2048], P(('seq', 'exp')), may hold values from -6 to 6
- expert_ids: int32 [16384, 2], P(('seq', 'exp')), may hold values from 0 to 63, all different within a row; in each aligned block of 64 rows (0 to 63, 64 to 127, ...) at most 2 rows name the same one
- route_weights: float32 [16384, 2], P(('seq', 'exp')), may hold values from 0.1 to 1
- gate_proj: bfloat16 [64, 1408, 4096], P('exp', 'seq'), may hold values from -0.09375 to 0.09375
- up_proj: bfloat16 [64, 1408, 4096], P('exp', 'seq'), may hold values from -0.09375 to 0.09375
- down_proj: bfloat16 [64, 1408, 4096], P('exp', 'seq'), may hold values from -0.15625 to 0.15625
Outputs:
- attention: bfloat16 [16384, 2048], P(('seq', 'exp'))
- expert_mix: bfloat16 [16384, 4096], P(('seq', 'exp'))
Inputs may be any that keep to these rules, and one draw needn't show every extreme that they name: `expert_ids`: the two experts of a token differ. Among the rows of one device (64 consecutive tokens, aligned), every expert is named exactly 2 times.
All inputs are finite; a program needn't handle non-finite values.
Results may differ from a plain program's by a relative error of at most 0.015.
Values may be sent and summed in bfloat16 or wider, within the bound.
A program may use at most 128 MiB of HBM per device.

v0:
```python
import math
import jax
import jax.numpy as jnp
from jax import lax
from jax.sharding import PartitionSpec as P

EXPERTS = 64
HDIM = 64
SUMS = 64
SEG_DEV = 2
CAP = 2
EPS = 1e-05
NEG = -1e30


def broadcast(value, axis, source):
    kept = jnp.where(lax.axis_index(axis) == source, value, 0).astype(value.dtype)
    return lax.psum(kept, axis)


def normalize(tokens, norm_gain):
    values = tokens.astype(jnp.float32)
    inv_rms = lax.rsqrt(jnp.mean(values * values, axis=-1, keepdims=True) + EPS)
    return (values * inv_rms * norm_gain).astype(jnp.bfloat16)


def attend_block(
    query_blk, seg_keys, seg_values, sum_keys, sum_values, first_row, segment, score_scale
):
    local_sc = (
        jnp.einsum("qhd,khd->hqk", query_blk, seg_keys, preferred_element_type=jnp.float32)
        * score_scale
    )
    summ_sc = (
        jnp.einsum("qhd,khd->hqk", query_blk, sum_keys, preferred_element_type=jnp.float32)
        * score_scale
    )
    query_pos = first_row + jnp.arange(query_blk.shape[0], dtype=jnp.int32)
    key_pos = jnp.arange(seg_keys.shape[0], dtype=jnp.int32)
    local_ok = key_pos[None, :] <= query_pos[:, None]
    summ_ok = jnp.arange(sum_keys.shape[0], dtype=jnp.int32) // SUMS < segment
    local_sc = jnp.where(local_ok[None], local_sc, NEG)
    summ_sc = jnp.where(summ_ok[None, None], summ_sc, NEG)
    top_sc = jnp.maximum(
        jnp.max(local_sc, axis=-1, keepdims=True), jnp.max(summ_sc, axis=-1, keepdims=True)
    )
    local_ex = jnp.exp(local_sc - top_sc)
    summ_ex = jnp.exp(summ_sc - top_sc)
    totals = jnp.sum(local_ex, axis=-1, keepdims=True) + jnp.sum(summ_ex, axis=-1, keepdims=True)
    local_wt = (local_ex / totals).astype(jnp.bfloat16)
    summ_wt = (summ_ex / totals).astype(jnp.bfloat16)
    mixed_out = jnp.einsum("hqk,khd->qhd", local_wt, seg_values, preferred_element_type=jnp.float32)
    return mixed_out + jnp.einsum(
        "hqk,khd->qhd", summ_wt, sum_values, preferred_element_type=jnp.float32
    )


def slot_table(id_rows):
    onehot = (id_rows[..., None] == jnp.arange(EXPERTS, dtype=jnp.int32)).astype(jnp.int32)
    before = jnp.cumsum(onehot, axis=-2) - onehot
    return jnp.sum(before * onehot, axis=-1)


def fill_slots(rows, slot_pos, slot_total):
    row_count = rows.shape[0]
    padded = jnp.concatenate([rows, jnp.zeros((1, rows.shape[1]), rows.dtype)], axis=0)
    source_row = jnp.arange(row_count * 2, dtype=jnp.int32) // 2
    index_table = jnp.full((slot_total,), row_count, jnp.int32).at[slot_pos].set(source_row)
    return padded[index_table]


def expert_block(row_block, gate_proj, up_proj, down_proj):
    gate_act = jnp.einsum(
        "...ecd,efd->...ecf", row_block, gate_proj, preferred_element_type=jnp.float32
    )
    up_act = jnp.einsum(
        "...ecd,efd->...ecf", row_block, up_proj, preferred_element_type=jnp.float32
    )
    hidden = (jax.nn.silu(gate_act) * up_act).astype(jnp.bfloat16)
    return jnp.einsum("...ecf,efd->...ecd", hidden, down_proj, preferred_element_type=jnp.float32)


def on_device(
    tokens,
    norm_gain,
    queries,
    attn_keys,
    attn_values,
    expert_ids,
    route_weights,
    gate_proj,
    up_proj,
    down_proj,
):
    exp_count = lax.axis_size("exp")
    seq_count = lax.axis_size("seq")
    local_tokens = tokens.shape[0]
    feature_count = tokens.shape[1]
    normed = normalize(tokens, norm_gain)
    head_q, head_k, head_v = (
        lax.all_to_all(queries, "exp", split_axis=1, concat_axis=0, tiled=True),
        lax.all_to_all(attn_keys, "exp", split_axis=1, concat_axis=0, tiled=True),
        lax.all_to_all(attn_values, "exp", split_axis=1, concat_axis=0, tiled=True),
    )
    heads_dev = head_q.shape[1] // HDIM
    seg_len = head_q.shape[0] // SEG_DEV
    block_len = seg_len // SUMS
    head_q = head_q.reshape(SEG_DEV, seg_len, heads_dev, HDIM)
    head_k = head_k.reshape(SEG_DEV, seg_len, heads_dev, HDIM)
    head_v = head_v.reshape(SEG_DEV, seg_len, heads_dev, HDIM)
    inv_block = 1.0 / math.sqrt(block_len)
    sum_k = (
        jnp.sum(
            head_k.astype(jnp.float32).reshape(SEG_DEV, SUMS, block_len, heads_dev, HDIM), axis=2
        )
        * inv_block
    ).astype(jnp.bfloat16)
    sum_v = (
        jnp.sum(
            head_v.astype(jnp.float32).reshape(SEG_DEV, SUMS, block_len, heads_dev, HDIM), axis=2
        )
        * inv_block
    ).astype(jnp.bfloat16)
    sum_k = sum_k.reshape(SEG_DEV * SUMS, heads_dev, HDIM)
    sum_v = sum_v.reshape(SEG_DEV * SUMS, heads_dev, HDIM)
    key_list = []
    value_list = []
    for root_index in range(seq_count):
        recv_keys, recv_values = (
            broadcast(sum_k, "seq", root_index),
            broadcast(sum_v, "seq", root_index),
        )
        key_list.append(recv_keys)
        value_list.append(recv_values)
    all_keys = jnp.concatenate(key_list, axis=0)
    all_values = jnp.concatenate(value_list, axis=0)
    query_rows = min(512, seg_len)
    score_scale = 1.0 / math.sqrt(HDIM)
    seg_base = lax.axis_index("seq") * SEG_DEV
    pieces = []
    for local_seg in range(SEG_DEV):
        for first_row in range(0, seg_len, query_rows):
            block_out = attend_block(
                head_q[local_seg, first_row : first_row + query_rows],
                head_k[local_seg],
                head_v[local_seg],
                all_keys,
                all_values,
                first_row,
                seg_base + local_seg,
                score_scale,
            )
            pieces.append(block_out.astype(jnp.bfloat16))
    head_out = jnp.concatenate(pieces, axis=0).reshape(SEG_DEV * seg_len, heads_dev * HDIM)
    attention = lax.all_to_all(head_out, "exp", split_axis=0, concat_axis=1, tiled=True)
    exp_dev = EXPERTS // exp_count
    flat_ids = expert_ids.reshape(-1)
    local_pos = flat_ids * CAP + slot_table(flat_ids)
    group_normed, group_ids = (
        lax.all_gather(normed, "seq", axis=0, tiled=True),
        lax.all_gather(expert_ids, "seq", axis=0, tiled=True),
    )
    id_rows = group_ids.reshape(seq_count, local_tokens * 2)
    slot_ids = slot_table(id_rows)
    source_ids = jnp.arange(seq_count, dtype=jnp.int32)[:, None]
    owner_dev = id_rows // exp_dev
    within = id_rows % exp_dev
    slot_pos = ((owner_dev * seq_count + source_ids) * exp_dev + within) * CAP + slot_ids
    send_rows = fill_slots(group_normed, slot_pos.reshape(-1), EXPERTS * seq_count * CAP)
    send_rows = send_rows.reshape(exp_count, seq_count, exp_dev, CAP, feature_count)
    recv_rows = lax.all_to_all(send_rows, "exp", split_axis=0, concat_axis=0, tiled=True)
    slice_term = expert_block(recv_rows, gate_proj, up_proj, down_proj)
    summed = lax.psum_scatter(
        slice_term.astype(jnp.bfloat16), "seq", scatter_dimension=1, tiled=True
    )
    owner_out = summed.reshape(exp_count, exp_dev * CAP, feature_count)
    source_out = lax.all_to_all(owner_out, "exp", split_axis=0, concat_axis=0, tiled=True).reshape(
        EXPERTS * CAP, feature_count
    )
    picked = source_out[local_pos].astype(jnp.float32).reshape(local_tokens, 2, feature_count)
    expert_mix = jnp.sum(route_weights[:, :, None] * picked, axis=1).astype(jnp.bfloat16)
    return (attention, expert_mix)


def solution(mesh):
    return jax.shard_map(
        on_device,
        mesh=mesh,
        in_specs=(
            P(("seq", "exp"), None),
            P(),
            P(("seq", "exp"), None),
            P(("seq", "exp"), None),
            P(("seq", "exp"), None),
            P(("seq", "exp"), None),
            P(("seq", "exp"), None),
            P("exp", "seq", None),
            P("exp", "seq", None),
            P("exp", "seq", None),
        ),
        out_specs=(P(("seq", "exp"), None), P(("seq", "exp"), None)),
        check_vma=False,
    )
```

profile of v0, /device:TPU:33, one launch (start us, length us, event | category | flops | bytes accessed | tf_op | source)
XLA Modules:
  0.0 657.0 jit_solution(4916319611330004537)
XLA Ops:
  7.2 1.4 fusion.51
  8.7 2.0 fusion.53
  10.7 1.3 all_to_all.62
  12.1 1.2 copy.142
  13.3 1.1 reshape.872
  14.4 10.9 %all-to-all-start.2 = ((bf16[32,2,2048]{2,1,0:T(2,128)(2,1)}), bf16[32,2,2048]{2,1,0:T(2,128)(2,1)}, u32[]{:S(2)}, u32[]{:S(2)}) async-start(bf16[32,2,2048]{2,1,0:T(2,128)(2,1)} %reshape.872), calls=%async_computation.2 | async-start | bytes 524288 | tf_op jit(solution)/shard_map/all_to_all | solution.py:103
  25.3 21.3 %all-gather = s32[8,64,2]{1,2,0:T(2,128)S(1)} all-gather(s32[1,64,2]{1,2,0:T(2,128)S(1)} %bitcast.256), channel_id=1, replica_groups=mesh['seq'=8,'exp'=32] {'seq'}, dimensions={0}, use_global_device_ids=true | all-gather | bytes 4608 | tf_op jit(solution)/shard_map/all_gather | solution.py:161
  46.7 0.9 copy.56
  47.7 2.3 all_to_all.59
  49.9 1.2 copy.143
  51.2 1.1 reshape.868
  52.3 1.1 reshape.827
  53.4 2.5 select_reduce_fusion
  56.0 11.4 %all-to-all-start.1 = ((bf16[32,2,2048]{2,1,0:T(2,128)(2,1)}), bf16[32,2,2048]{2,1,0:T(2,128)(2,1)S(1)}, u32[]{:S(2)}, u32[]{:S(2)}) async-start(bf16[32,2,2048]{2,1,0:T(2,128)(2,1)} %reshape.868), calls=%async_computation.1 | async-start | bytes 524288 | tf_op jit(solution)/shard_map/all_to_all | solution.py:102
  67.5 4.3 scatter_custom_fusion
  71.8 45.0 %all-gather.3.cloned.1.call-done = bf16[512,4096]{1,0:T(8,128)(2,1)} async-done(((bf16[64,4096]{1,0:T(8,128)(2,1)}), bf16[512,4096]{1,0:T(8,128)(2,1)}) %all-gather.3.cloned.1.call-update) | async-done | bytes 4194320 | tf_op jit(solution)/shard_map/all_gather | solution.py:160
  116.8 4.7 concatenate.15
  121.5 17.8 %gather_fusion = bf16[1024,4096]{1,0:T(8,128)(2,1)} fusion(bf16[513,4096]{1,0:T(8,128)(2,1)} %concatenate.15, s32[1024]{0:T(1024)S(1)} %fusion.100), kind=kCustom, calls=%fused_computation | custom fusion | bytes 16781312 | tf_op jit(solution)/shard_map/gather | solution.py:69
  139.4 14.3 %reshape.828 = bf16[32,8,2,2,4096]{4,3,2,1,0:T(2,128)(2,1)} reshape(bf16[1024,4096]{1,0:T(8,128)(2,1)} %gather_fusion) | data formatting | bytes 16777216 | tf_op jit(solution)/shard_map/reshape | solution.py:170
  153.7 16.3 %copy.59 = bf16[32,8,2,2,4096]{4,1,3,2,0:T(8,128)(2,1)} copy(bf16[32,8,2,2,4096]{4,3,2,1,0:T(2,128)(2,1)} %reshape.828) | data formatting | bytes 16777216 | tf_op jit(solution)/shard_map/reshape | solution.py:170
  170.7 10.5 %all-to-all-start.4 = ((bf16[32,8,2,2,4096]{4,1,3,2,0:T(8,128)(2,1)}), bf16[32,8,2,2,4096]{4,1,3,2,0:T(8,128)(2,1)}, u32[]{:S(2)}, u32[]{:S(2)}) async-start(bf16[32,8,2,2,4096]{4,1,3,2,0:T(8,128)(2,1)} %copy.59), calls=%async_computation.4 | async-start | bytes 16777216 | tf_op jit(solution)/shard_map/all_to_all | solution.py:171
  181.3 1.3 reshape.873
  182.6 2.1 reshape.869
  184.9 1.3 convert_reduce_fusion.1
  187.6 0.7 broadcast_select_fusion.2
  188.7 198.8 %all-to-all-done.4 = bf16[32,8,2,2,4096]{4,1,3,2,0:T(8,128)(2,1)} async-done(((bf16[32,8,2,2,4096]{4,1,3,2,0:T(8,128)(2,1)}), bf16[32,8,2,2,4096]{4,1,3,2,0:T(8,128)(2,1)}, u32[]{:S(2)}, u32[]{:S(2)}) %all-to-all-start.4) | async-done | bytes 8388640 | tf_op jit(solution)/shard_map/all_to_all | solution.py:171
  387.6 6.7 %fusion.19 = f32[32,8,2,2,176]{4,1,3,0,2:T(8,128)S(1)} fusion(bf16[2,176,4096]{2,1,0:T(8,128)(2,1)} %param.17, bf16[32,8,2,2,4096]{4,1,3,2,0:T(8,128)(2,1)} %all-to-all-done.4), kind=kOutput, calls=%fused_computation.50 | convolution fusion | flops 1476395008 | bytes 11993088 | tf_op jit(solution)/shard_map/...ecd,efd->...ecf/dot_general | solution.py:73
  394.3 6.0 fusion.34
  400.3 5.5 convert_bitcast_fusion
  405.9 11.4 %copy.62 = bf16[32,8,2,2,4096]{4,0,3,2,1:T(8,128)(2,1)} copy(bf16[32,8,2,2,4096]{4,1,3,0,2:T(8,128)(2,1)} %convert_bitcast_fusion) | data formatting | bytes 16777216 | tf_op jit(solution)/shard_map/convert_element_type | solution.py:174
  417.2 0.9 copy-done.9
  418.4 1.1 reshape.870
  419.6 4.8 all-to-all-start
  424.4 16.2 %all-to-all-done = bf16[32,2,2048]{2,1,0:T(2,128)(2,1)S(1)} async-done(((bf16[32,2,2048]{2,1,0:T(2,128)(2,1)}), bf16[32,2,2048]{2,1,0:T(2,128)(2,1)S(1)}, u32[]{:S(2)}, u32[]{:S(2)}) %all-to-all-start) | async-done | bytes 262176 | tf_op jit(solution)/shard_map/all_to_all | solution.py:101
  442.3 1.8 fusion.118
  444.2 1.9 fusion.116
  446.1 1.9 fusion.117
  448.0 1.9 fusion.115
  449.8 0.9 constant_dynamic-update-slice_fusion.7
  450.7 0.8 constant_dynamic-update-slice_fusion.6
  451.5 0.8 constant_dynamic-update-slice_fusion.5
  452.3 0.8 constant_dynamic-update-slice_fusion.4
  453.0 0.8 constant_dynamic-update-slice_fusion.3
  453.8 0.8 constant_dynamic-update-slice_fusion.2
  454.6 0.8 constant_dynamic-update-slice_fusion.1
  455.3 0.8 constant_dynamic-update-slice_fusion
  457.1 0.8 fusion.15
  457.9 0.8 copy-done.5
  461.3 0.8 fusion.17
  462.1 0.8 copy-done.3
  464.2 0.8 fusion.54
  465.6 0.8 fusion.55
  467.0 0.8 fusion.56
  468.4 1.0 fusion.57
  470.8 1.1 reshape.874
  471.9 4.3 all-to-all-start.3
  476.2 119.8 %reduce-scatter.2.cloned.1.call-done = bf16[32,1,2,2,4096]{4,0,3,2,1:T(8,128)(2,1)} async-done(((bf16[32,8,2,2,4096]{4,0,3,2,1:T(8,128)(2,1)}), bf16[32,1,2,2,4096]{4,0,3,2,1:T(8,128)(2,1)}) %reduce-scatter.2.cloned.1.call-update) | async-done | bytes 1048592 | tf_op jit(solution)/shard_map/reduce_scatter | solution.py:173
  596.0 3.0 copy.63
  599.1 9.9 %all-to-all-start.5 = ((bf16[32,4,4096]{2,1,0:T(4,128)(2,1)}), bf16[32,4,4096]{2,1,0:T(4,128)(2,1)S(1)}, u32[]{:S(2)}, u32[]{:S(2)}) async-start(bf16[32,4,4096]{2,1,0:T(4,128)(2,1)} %copy.63), calls=%async_computation.6 | async-start | bytes 2097152 | tf_op jit(solution)/shard_map/all_to_all | solution.py:177
  610.4 0.9 copy.66
  611.3 27.4 %all-to-all-done.5 = bf16[32,4,4096]{2,1,0:T(4,128)(2,1)S(1)} async-done(((bf16[32,4,4096]{2,1,0:T(4,128)(2,1)}), bf16[32,4,4096]{2,1,0:T(4,128)(2,1)S(1)}, u32[]{:S(2)}, u32[]{:S(2)}) %all-to-all-start.5) | async-done | bytes 1048608 | tf_op jit(solution)/shard_map/all_to_all | solution.py:177
  639.0 2.2 gather_fusion.1
  641.2 3.5 reshape.833
  644.7 5.6 multiply_reduce_fusion
  (120 shorter events, 14.6 us)
Async XLA Ops:
  7.2 393.1 %copy-start = (bf16[2,176,4096]{2,1,0:T(8,128)(2,1)S(1)}, bf16[2,176,4096]{2,1,0:T(8,128)(2,1)}, u32[]{:S(2)}) copy-start(bf16[2,176,4096]{2,1,0:T(8,128)(2,1)} %param.19) | copy-start | bytes 8650756
  7.2 3.6 copy-start.8
  7.2 109.6 %all-gather.3.cloned.1.call-start = ((), (), s32[]{:S(2)}) async-start(), calls=%async_computation.7 | async-start | bytes 4718592 | tf_op jit(solution)/shard_map/all_gather | solution.py:160
  10.7 14.6 %copy-start.20 = (s32[64,2]{0,1:T(2,128)S(1)}, s32[64,2]{0,1:T(2,128)}, u32[]{:S(2)}) copy-start(s32[64,2]{0,1:T(2,128)} %param.15) | copy-start | bytes 1540
  14.4 41.6 %all-to-all-start.2 = ((bf16[32,2,2048]{2,1,0:T(2,128)(2,1)}), bf16[32,2,2048]{2,1,0:T(2,128)(2,1)}, u32[]{:S(2)}, u32[]{:S(2)}) async-start(bf16[32,2,2048]{2,1,0:T(2,128)(2,1)} %reshape.872), calls=%async_computation.2 | async-start | bytes 524288 | tf_op jit(solution)/shard_map/all_to_all | solution.py:103
  56.0 114.0 %all-to-all-start.1 = ((bf16[32,2,2048]{2,1,0:T(2,128)(2,1)}), bf16[32,2,2048]{2,1,0:T(2,128)(2,1)S(1)}, u32[]{:S(2)}, u32[]{:S(2)}) async-start(bf16[32,2,2048]{2,1,0:T(2,128)(2,1)} %reshape.868), calls=%async_computation.1 | async-start | bytes 524288 | tf_op jit(solution)/shard_map/all_to_all | solution.py:102
  170.0 0.7 copy-start.7
  170.7 216.9 %all-to-all-start.4 = ((bf16[32,8,2,2,4096]{4,1,3,2,0:T(8,128)(2,1)}), bf16[32,8,2,2,4096]{4,1,3,2,0:T(8,128)(2,1)}, u32[]{:S(2)}, u32[]{:S(2)}) async-start(bf16[32,8,2,2,4096]{4,1,3,2,0:T(8,128)(2,1)} %copy.59), calls=%async_computation.4 | async-start | bytes 16777216 | tf_op jit(solution)/shard_map/all_to_all | solution.py:171
  181.2 268.6 %all-reduce.4.cloned.1.call-start = ((), (), s32[]{:S(2)}) async-start(), calls=%async_computation.9 | async-start | bytes 1048576 | tf_op jit(solution)/shard_map/psum | solution.py:18
  188.3 407.7 %reduce-scatter.2.cloned.1.call-start = ((), (), s32[]{:S(2)}) async-start(), calls=%async_computation.8 | async-start | bytes 9437184 | tf_op jit(solution)/shard_map/reduce_scatter | solution.py:173
  387.6 6.7 %copy-start.22 = (bf16[2,176,4096]{2,1,0:T(8,128)(2,1)S(1)}, bf16[2,176,4096]{2,1,0:T(8,128)(2,1)}, u32[]{:S(2)}) copy-start(bf16[2,176,4096]{2,1,0:T(8,128)(2,1)} %param.18) | copy-start | bytes 8650756
  417.2 0.9 copy-start.9
  419.6 21.1 %all-to-all-start = ((bf16[32,2,2048]{2,1,0:T(2,128)(2,1)}), bf16[32,2,2048]{2,1,0:T(2,128)(2,1)S(1)}, u32[]{:S(2)}, u32[]{:S(2)}) async-start(bf16[32,2,2048]{2,1,0:T(2,128)(2,1)} %reshape.870), calls=%async_computation | async-start | bytes 524288 | tf_op jit(solution)/shard_map/all_to_all | solution.py:101
  441.0 1.1 copy-start.2
  442.1 3.9 copy-start.10
  449.8 6.7 %copy-start.6 = (f32[512,1024]{1,0:T(8,128)S(1)}, f32[512,1024]{1,0:T(8,128)}, u32[]{:S(2)}) copy-start(f32[512,1024]{1,0:T(8,128)} %get-tuple-element.60) | copy-start | bytes 6291460
  456.1 1.0 copy-start.11
  457.1 1.6 copy-start.5
  459.2 1.6 copy-start.4
  461.3 1.6 copy-start.3
  462.9 1.1 copy-start.19
  462.9 1.1 copy-start.18
  462.9 1.1 copy-start.17
  462.9 1.2 copy-start.16
  462.9 1.2 copy-start.15
  462.9 1.2 copy-start.14
  462.9 1.2 copy-start.13
  462.9 1.2 copy-start.12
  471.9 127.2 %all-to-all-start.3 = ((bf16[32,2,2048]{2,1,0:T(2,128)(2,1)}), bf16[32,2,2048]{2,1,0:T(2,128)(2,1)S(1)}, u32[]{:S(2)}, u32[]{:S(2)}) async-start(bf16[32,2,2048]{2,1,0:T(2,128)(2,1)} %reshape.874), calls=%async_computation.3 | async-start | bytes 524288 | tf_op jit(solution)/shard_map/all_to_all | solution.py:155
  596.0 13.7 %copy-start.21 = (f32[64,2]{0,1:T(2,128)S(1)}, f32[64,2]{0,1:T(2,128)}, u32[]{:S(2)}) copy-start(f32[64,2]{0,1:T(2,128)} %param.16) | copy-start | bytes 1540
  599.1 39.7 %all-to-all-start.5 = ((bf16[32,4,4096]{2,1,0:T(4,128)(2,1)}), bf16[32,4,4096]{2,1,0:T(4,128)(2,1)S(1)}, u32[]{:S(2)}, u32[]{:S(2)}) async-start(bf16[32,4,4096]{2,1,0:T(4,128)(2,1)} %copy.63), calls=%async_computation.6 | async-start | bytes 2097152 | tf_op jit(solution)/shard_map/all_to_all | solution.py:177
  641.2 9.1 %copy-start.1 = (bf16[2,176,4096]{2,1,0:T(8,128)(2,1)S(1)}, bf16[2,176,4096]{2,1,0:T(8,128)(2,1)}, u32[]{:S(2)}) copy-start(bf16[2,176,4096]{2,1,0:T(8,128)(2,1)} %param.19) | copy-start | bytes 8650756
Sparse Core Ops, SparseCore 0:
  10.8 105.9 all-gather.2
  188.4 129.2 all-reduce.3
  417.4 178.6 reduce-scatter.1
where the time goes:
time: 666 us; the launch traced here: 657 us
  waiting for transfers between devices  407 us (61%)
  local copies, waits for them, and re-layouts  109 us (16%)
  starting transfers between devices  52.4 us (8%)
  matrix products  33.9 us (5%)
  blocking collectives  21.3 us (3%)
  other arithmetic  18.7 us (3%)
  between operations  14.7 us (2%)
    all_to_all x1, waiting for transfers between devices, on_device(): lax.all_to_all(send_rows, 'exp', split_axis=0, concat_axis=0, tiled=True)  199 us
    reduce_scatter x1, waiting for transfers between devices, on_device(): lax.psum_scatter(slice_term.astype(jnp.bfloat16), 'seq', scatter_dimensio...  120 us
    all_gather x1, waiting for transfers between devices, on_device(): lax.all_gather(normed, 'seq', axis=0, tiled=True)  45 us
    reshape x2, local copies, waits for them, and re-layouts, on_device(): send_rows.reshape(exp_count, seq_count, exp_dev, CAP, feature_count)  30.6 us
    all_to_all x1, waiting for transfers between devices, on_device(): lax.all_to_all(owner_out, 'exp', split_axis=0, concat_axis=0, tiled=True)  27.4 us
    all_gather x1, blocking collectives, on_device(): lax.all_gather(expert_ids, 'seq', axis=0, tiled=True)  21.3 us
    unnamed x72, local copies, waits for them, and re-layouts  19.5 us
    gather x1, local copies, waits for them, and re-layouts, fill_slots(): return padded[index_table]  17.8 us
  transfers between devices with their start and end apart: 9, of which 5 were waited for; matrix products, arithmetic and copies ran while one was open for 21% of the time, Pallas kernels for 0%

commit v1 on v0

--- a/solution.py
+++ b/solution.py
@@ -158,7 +158,9 @@
     local_pos = flat_ids * CAP + slot_table(flat_ids)
     group_normed, group_ids = (
         lax.all_gather(normed, "seq", axis=0, tiled=True),
-        lax.all_gather(expert_ids, "seq", axis=0, tiled=True),
+        jnp.concatenate(
+            lax.all_to_all(jnp.stack([expert_ids] * lax.axis_size("seq")), "seq", 0, 0), axis=0
+        ),
     )
     id_rows = group_ids.reshape(seq_count, local_tokens * 2)
     slot_ids = slot_table(id_rows)

time: 666 us -> 666 us (level)
  waiting for transfers between devices: 407 us -> 429 us
  blocking collectives: 21.3 us -> 0 us
    all_gather x1 -> x0, blocking collectives: 21.3 us -> none  [on_device(): lax.all_gather(expert_ids, 'seq', axis=0, tiled=True)]
    all_to_all x1, waiting for transfers between devices: 0.01 us -> 10.9 us  [on_device(): lax.all_to_all(attn_values, 'exp', split_axis=1, concat_axis=0, tiled=True)]
    all_gather x1, waiting for transfers between devices: 45 us -> 55 us  [on_device(): lax.all_gather(normed, 'seq', axis=0, tiled=True)]
    all_to_all x1, starting transfers between devices: 11.4 us -> 4.49 us  [on_device(): lax.all_to_all(attn_keys, 'exp', split_axis=1, concat_axis=0, tiled=True)]
    unnamed x72 -> x75, local copies, waits for them, and re-layouts: 19.5 us -> 20.2 us
  transfers between devices with their start and end apart: 9 -> 10, of which waited for: 5 -> 7; matrix products, arithmetic and copies ran while one was open for 21% -> 21% of each run, Pallas kernels for 0% -> 0%
where the time goes in v1:
time: 666 us; the launch traced here: 657 us
  waiting for transfers between devices  429 us (64%)
  local copies, waits for them, and re-layouts  108 us (16%)
  starting transfers between devices  52.3 us (8%)
  matrix products  33.9 us (5%)
  other arithmetic  19.2 us (3%)
  between operations  14.7 us (2%)
    all_to_all x1, waiting for transfers between devices, on_device(): lax.all_to_all(send_rows, 'exp', split_axis=0, concat_axis=0, tiled=True)  199 us
    reduce_scatter x1, waiting for transfers between devices, on_device(): lax.psum_scatter(slice_term.astype(jnp.bfloat16), 'seq', scatter_dimensio...  120 us
    all_gather x1, waiting for transfers between devices, on_device(): lax.all_gather(normed, 'seq', axis=0, tiled=True)  55 us
    reshape x2, local copies, waits for them, and re-layouts, on_device(): send_rows.reshape(exp_count, seq_count, exp_dev, CAP, feature_count)  30.6 us
    all_to_all x1, waiting for transfers between devices, on_device(): lax.all_to_all(owner_out, 'exp', split_axis=0, concat_axis=0, tiled=True)  27.4 us
    unnamed x75, local copies, waits for them, and re-layouts  20.2 us
    gather x1, local copies, waits for them, and re-layouts, fill_slots(): return padded[index_table]  17.8 us
    all_to_all x1, waiting for transfers between devices, on_device(): lax.all_to_all(queries, 'exp', split_axis=1, concat_axis=0, tiled=True)  16.2 us
  transfers between devices with their start and end apart: 10, of which 7 were waited for; matrix products, arithmetic and copies ran while one was open for 21% of the time, Pallas kernels for 0%

profile of v1, /device:TPU:33, one launch (start us, length us, event | category | flops | bytes accessed | tf_op | source)
XLA Modules:
  0.0 656.9 jit_solution(3503397108101651961)
XLA Ops:
  7.2 1.4 fusion.51
  8.7 2.0 fusion.53
  11.4 5.4 all-to-all-start.4
  16.8 1.3 all_to_all.65
  18.1 1.2 copy.143
  19.3 1.1 reshape.868
  20.6 12.3 %all-to-all-start.2 = ((bf16[32,2,2048]{2,1,0:T(2,128)(2,1)}), bf16[32,2,2048]{2,1,0:T(2,128)(2,1)}, u32[]{:S(2)}, u32[]{:S(2)}) async-start(bf16[32,2,2048]{2,1,0:T(2,128)(2,1)} %reshape.868), calls=%async_computation.2 | async-start | bytes 524288 | tf_op jit(solution)/shard_map/all_to_all | solution.py:103
  33.0 2.3 all_to_all.62
  35.3 1.3 copy.144
  36.5 1.1 reshape.864
  38.9 10.9 %all-to-all-done.2 = bf16[32,2,2048]{2,1,0:T(2,128)(2,1)} async-done(((bf16[32,2,2048]{2,1,0:T(2,128)(2,1)}), bf16[32,2,2048]{2,1,0:T(2,128)(2,1)}, u32[]{:S(2)}, u32[]{:S(2)}) %all-to-all-start.2) | async-done | bytes 262176 | tf_op jit(solution)/shard_map/all_to_all | solution.py:103
  49.8 4.5 all-to-all-start.1
  54.3 2.5 select_reduce_fusion
  57.3 4.3 scatter_custom_fusion
  61.6 55.0 %all-gather.2.cloned.1.call-done = bf16[512,4096]{1,0:T(8,128)(2,1)} async-done(((bf16[64,4096]{1,0:T(8,128)(2,1)}), bf16[512,4096]{1,0:T(8,128)(2,1)}) %all-gather.2.cloned.1.call-update) | async-done | bytes 4194320 | tf_op jit(solution)/shard_map/all_gather | solution.py:160
  116.7 4.7 concatenate.15
  121.4 17.8 %gather_fusion = bf16[1024,4096]{1,0:T(8,128)(2,1)} fusion(bf16[513,4096]{1,0:T(8,128)(2,1)} %concatenate.15, s32[1024]{0:T(1024)S(1)} %fusion.100), kind=kCustom, calls=%fused_computation | custom fusion | bytes 16781312 | tf_op jit(solution)/shard_map/gather | solution.py:69
  139.2 14.3 %reshape.826 = bf16[32,8,2,2,4096]{4,3,2,1,0:T(2,128)(2,1)} reshape(bf16[1024,4096]{1,0:T(8,128)(2,1)} %gather_fusion) | data formatting | bytes 16777216 | tf_op jit(solution)/shard_map/reshape | solution.py:172
  153.5 16.3 %copy.60 = bf16[32,8,2,2,4096]{4,1,3,2,0:T(8,128)(2,1)} copy(bf16[32,8,2,2,4096]{4,3,2,1,0:T(2,128)(2,1)} %reshape.826) | data formatting | bytes 16777216 | tf_op jit(solution)/shard_map/reshape | solution.py:172
  169.8 0.7 copy-done.7
  170.5 10.5 %all-to-all-start.5 = ((bf16[32,8,2,2,4096]{4,1,3,2,0:T(8,128)(2,1)}), bf16[32,8,2,2,4096]{4,1,3,2,0:T(8,128)(2,1)}, u32[]{:S(2)}, u32[]{:S(2)}) async-start(bf16[32,8,2,2,4096]{4,1,3,2,0:T(8,128)(2,1)} %copy.60), calls=%async_computation.5 | async-start | bytes 16777216 | tf_op jit(solution)/shard_map/all_to_all | solution.py:173
  181.1 1.3 reshape.869
  182.4 2.1 reshape.865
  184.8 1.3 convert_reduce_fusion.1
  187.4 0.7 broadcast_select_fusion.2
  188.6 198.8 %all-to-all-done.5 = bf16[32,8,2,2,4096]{4,1,3,2,0:T(8,128)(2,1)} async-done(((bf16[32,8,2,2,4096]{4,1,3,2,0:T(8,128)(2,1)}), bf16[32,8,2,2,4096]{4,1,3,2,0:T(8,128)(2,1)}, u32[]{:S(2)}, u32[]{:S(2)}) %all-to-all-start.5) | async-done | bytes 8388640 | tf_op jit(solution)/shard_map/all_to_all | solution.py:173
  387.4 6.7 %fusion.19 = f32[32,8,2,2,176]{4,1,3,0,2:T(8,128)S(1)} fusion(bf16[2,176,4096]{2,1,0:T(8,128)(2,1)} %param.17, bf16[32,8,2,2,4096]{4,1,3,2,0:T(8,128)(2,1)} %all-to-all-done.5), kind=kOutput, calls=%fused_computation.50 | convolution fusion | flops 1476395008 | bytes 11993088 | tf_op jit(solution)/shard_map/...ecd,efd->...ecf/dot_general | solution.py:73
  394.1 6.0 fusion.34
  400.2 5.5 convert_bitcast_fusion
  405.7 11.4 %copy.63 = bf16[32,8,2,2,4096]{4,0,3,2,1:T(8,128)(2,1)} copy(bf16[32,8,2,2,4096]{4,1,3,0,2:T(8,128)(2,1)} %convert_bitcast_fusion) | data formatting | bytes 16777216 | tf_op jit(solution)/shard_map/convert_element_type | solution.py:176
  417.1 0.9 copy-done.9
  418.3 1.1 reshape.866
  419.4 4.8 all-to-all-start
  424.3 16.2 %all-to-all-done = bf16[32,2,2048]{2,1,0:T(2,128)(2,1)S(1)} async-done(((bf16[32,2,2048]{2,1,0:T(2,128)(2,1)}), bf16[32,2,2048]{2,1,0:T(2,128)(2,1)S(1)}, u32[]{:S(2)}, u32[]{:S(2)}) %all-to-all-start) | async-done | bytes 262176 | tf_op jit(solution)/shard_map/all_to_all | solution.py:101
  442.2 1.9 fusion.118
  444.0 1.9 fusion.116
  445.9 1.9 fusion.117
  447.8 1.9 fusion.115
  449.7 0.9 constant_dynamic-update-slice_fusion.7
  450.6 0.8 constant_dynamic-update-slice_fusion.6
  451.3 0.8 constant_dynamic-update-slice_fusion.5
  452.1 0.8 constant_dynamic-update-slice_fusion.4
  452.9 0.8 constant_dynamic-update-slice_fusion.3
  453.6 0.8 constant_dynamic-update-slice_fusion.2
  454.4 0.8 constant_dynamic-update-slice_fusion.1
  455.2 0.8 constant_dynamic-update-slice_fusion
  456.9 0.8 fusion.15
  457.7 0.8 copy-done.5
  461.1 0.8 fusion.17
  461.9 0.8 copy-done.3
  464.0 0.8 fusion.54
  465.4 0.8 fusion.55
  466.8 0.8 fusion.56
  468.2 1.0 fusion.57
  470.6 1.1 reshape.870
  471.7 4.3 all-to-all-start.3
  476.0 119.8 %reduce-scatter.2.cloned.1.call-done = bf16[32,1,2,2,4096]{4,0,3,2,1:T(8,128)(2,1)} async-done(((bf16[32,8,2,2,4096]{4,0,3,2,1:T(8,128)(2,1)}), bf16[32,1,2,2,4096]{4,0,3,2,1:T(8,128)(2,1)}) %reduce-scatter.2.cloned.1.call-update) | async-done | bytes 1048592 | tf_op jit(solution)/shard_map/reduce_scatter | solution.py:175
  595.8 3.0 copy.64
  598.9 10.0 %all-to-all-start.6 = ((bf16[32,4,4096]{2,1,0:T(4,128)(2,1)}), bf16[32,4,4096]{2,1,0:T(4,128)(2,1)S(1)}, u32[]{:S(2)}, u32[]{:S(2)}) async-start(bf16[32,4,4096]{2,1,0:T(4,128)(2,1)} %copy.64), calls=%async_computation.7 | async-start | bytes 2097152 | tf_op jit(solution)/shard_map/all_to_all | solution.py:179
  610.3 0.9 copy.67
  611.2 27.4 %all-to-all-done.6 = bf16[32,4,4096]{2,1,0:T(4,128)(2,1)S(1)} async-done(((bf16[32,4,4096]{2,1,0:T(4,128)(2,1)}), bf16[32,4,4096]{2,1,0:T(4,128)(2,1)S(1)}, u32[]{:S(2)}, u32[]{:S(2)}) %all-to-all-start.6) | async-done | bytes 1048608 | tf_op jit(solution)/shard_map/all_to_all | solution.py:179
  638.9 2.2 gather_fusion.1
  641.0 3.5 reshape.831
  644.6 5.6 multiply_reduce_fusion
  (126 shorter events, 16.2 us)
Async XLA Ops:
  7.2 393.0 %copy-start = (bf16[2,176,4096]{2,1,0:T(8,128)(2,1)S(1)}, bf16[2,176,4096]{2,1,0:T(8,128)(2,1)}, u32[]{:S(2)}) copy-start(bf16[2,176,4096]{2,1,0:T(8,128)(2,1)} %param.19) | copy-start | bytes 8650756
  7.2 3.5 copy-start.20
  7.2 9.6 %copy-start.8 = (bf16[64,2048]{1,0:T(8,128)(2,1)S(1)}, bf16[64,2048]{1,0:T(8,128)(2,1)}, u32[]{:S(2)}) copy-start(bf16[64,2048]{1,0:T(8,128)(2,1)} %param.14) | copy-start | bytes 786436
  7.2 109.5 %all-gather.2.cloned.1.call-start = ((), (), s32[]{:S(2)}) async-start(), calls=%async_computation.8 | async-start | bytes 4718592 | tf_op jit(solution)/shard_map/all_gather | solution.py:160
  11.4 9.2 %all-to-all-start.4 = ((s32[8,1,128]{2,1,0:T(1,128)}), s32[8,1,128]{2,1,0:T(1,128)S(1)}, u32[]{:S(2)}, u32[]{:S(2)}) async-start(s32[8,1,128]{2,1,0:T(1,128)} %reshape.862), calls=%async_computation.4 | async-start | bytes 8192 | tf_op jit(solution)/shard_map/all_to_all | solution.py:162
  20.6 29.1 %all-to-all-start.2 = ((bf16[32,2,2048]{2,1,0:T(2,128)(2,1)}), bf16[32,2,2048]{2,1,0:T(2,128)(2,1)}, u32[]{:S(2)}, u32[]{:S(2)}) async-start(bf16[32,2,2048]{2,1,0:T(2,128)(2,1)} %reshape.868), calls=%async_computation.2 | async-start | bytes 524288 | tf_op jit(solution)/shard_map/all_to_all | solution.py:103
  49.8 120.0 %all-to-all-start.1 = ((bf16[32,2,2048]{2,1,0:T(2,128)(2,1)}), bf16[32,2,2048]{2,1,0:T(2,128)(2,1)S(1)}, u32[]{:S(2)}, u32[]{:S(2)}) async-start(bf16[32,2,2048]{2,1,0:T(2,128)(2,1)} %reshape.864), calls=%async_computation.1 | async-start | bytes 524288 | tf_op jit(solution)/shard_map/all_to_all | solution.py:102
  169.8 0.7 copy-start.7
  170.5 216.9 %all-to-all-start.5 = ((bf16[32,8,2,2,4096]{4,1,3,2,0:T(8,128)(2,1)}), bf16[32,8,2,2,4096]{4,1,3,2,0:T(8,128)(2,1)}, u32[]{:S(2)}, u32[]{:S(2)}) async-start(bf16[32,8,2,2,4096]{4,1,3,2,0:T(8,128)(2,1)} %copy.60), calls=%async_computation.5 | async-start | bytes 16777216 | tf_op jit(solution)/shard_map/all_to_all | solution.py:173
  181.0 268.6 %all-reduce.4.cloned.1.call-start = ((), (), s32[]{:S(2)}) async-start(), calls=%async_computation.10 | async-start | bytes 1048576 | tf_op jit(solution)/shard_map/psum | solution.py:18
  188.1 407.7 %reduce-scatter.2.cloned.1.call-start = ((), (), s32[]{:S(2)}) async-start(), calls=%async_computation.9 | async-start | bytes 9437184 | tf_op jit(solution)/shard_map/reduce_scatter | solution.py:175
  387.4 6.7 %copy-start.22 = (bf16[2,176,4096]{2,1,0:T(8,128)(2,1)S(1)}, bf16[2,176,4096]{2,1,0:T(8,128)(2,1)}, u32[]{:S(2)}) copy-start(bf16[2,176,4096]{2,1,0:T(8,128)(2,1)} %param.18) | copy-start | bytes 8650756
  417.1 0.9 copy-start.9
  419.4 21.1 %all-to-all-start = ((bf16[32,2,2048]{2,1,0:T(2,128)(2,1)}), bf16[32,2,2048]{2,1,0:T(2,128)(2,1)S(1)}, u32[]{:S(2)}, u32[]{:S(2)}) async-start(bf16[32,2,2048]{2,1,0:T(2,128)(2,1)} %reshape.866), calls=%async_computation | async-start | bytes 524288 | tf_op jit(solution)/shard_map/all_to_all | solution.py:101
  440.9 1.1 copy-start.2
  442.0 3.9 copy-start.10
  449.7 6.7 %copy-start.6 = (f32[512,1024]{1,0:T(8,128)S(1)}, f32[512,1024]{1,0:T(8,128)}, u32[]{:S(2)}) copy-start(f32[512,1024]{1,0:T(8,128)} %get-tuple-element.60) | copy-start | bytes 6291460
  455.9 1.0 copy-start.11
  456.9 1.6 copy-start.5
  459.0 1.6 copy-start.4
  461.1 1.6 copy-start.3
  462.7 1.1 copy-start.19
  462.7 1.1 copy-start.18
  462.7 1.1 copy-start.17
  462.7 1.2 copy-start.16
  462.8 1.2 copy-start.15
  462.8 1.2 copy-start.14
  462.8 1.2 copy-start.13
  462.8 1.2 copy-start.12
  471.7 127.2 %all-to-all-start.3 = ((bf16[32,2,2048]{2,1,0:T(2,128)(2,1)}), bf16[32,2,2048]{2,1,0:T(2,128)(2,1)S(1)}, u32[]{:S(2)}, u32[]{:S(2)}) async-start(bf16[32,2,2048]{2,1,0:T(2,128)(2,1)} %reshape.870), calls=%async_computation.3 | async-start | bytes 524288 | tf_op jit(solution)/shard_map/all_to_all | solution.py:155
  595.8 13.8 %copy-start.21 = (f32[64,2]{0,1:T(2,128)S(1)}, f32[64,2]{0,1:T(2,128)}, u32[]{:S(2)}) copy-start(f32[64,2]{0,1:T(2,128)} %param.16) | copy-start | bytes 1540
  598.9 39.7 %all-to-all-start.6 = ((bf16[32,4,4096]{2,1,0:T(4,128)(2,1)}), bf16[32,4,4096]{2,1,0:T(4,128)(2,1)S(1)}, u32[]{:S(2)}, u32[]{:S(2)}) async-start(bf16[32,4,4096]{2,1,0:T(4,128)(2,1)} %copy.64), calls=%async_computation.7 | async-start | bytes 2097152 | tf_op jit(solution)/shard_map/all_to_all | solution.py:179
  641.0 9.1 %copy-start.1 = (bf16[2,176,4096]{2,1,0:T(8,128)(2,1)S(1)}, bf16[2,176,4096]{2,1,0:T(8,128)(2,1)}, u32[]{:S(2)}) copy-start(bf16[2,176,4096]{2,1,0:T(8,128)(2,1)} %param.19) | copy-start | bytes 8650756
Sparse Core Ops, SparseCore 0:
  10.8 105.7 all-gather.1
  188.2 129.1 all-reduce.3
  417.2 178.5 reduce-scatter.1
